TPU v7x, 32 devices: a whole 2x2x4 slice. The times are simulated.
32 devices in a mesh: tm: 16 (over z, y, x), tile: 2 (over core).
Axes of the slice: x: 2, y: 2, z: 4, core: 2. Of those that a mesh axis runs over, the one named last changes fastest.
Arguments:
- latent: bfloat16 [64, 8, 160, 128], P('tm', 'tile'), may hold values from -6 to 6
- cot_forward: bfloat16 [64, 8, 160, 128], P('tm', 'tile'), may hold values from -6 to 6
- cot_reverse: bfloat16 [64, 8, 160, 128], P('tm', 'tile'), may hold values from -6 to 6
- spatial_weight: bfloat16 [3, 3, 128, 128], replicated, may hold values from -0.1875 to 0.1875
- temporal_weight: bfloat16 [3, 128, 128], replicated, may hold values from -0.3125 to 0.3125
Outputs:
- out_forward: bfloat16 [64, 8, 160, 128], P('tm', 'tile')
- out_reverse: bfloat16 [64, 8, 160, 128], P('tm', 'tile')
- grad_input: bfloat16 [64, 8, 160, 128], P('tm', 'tile')
- grad_spatial: float32 [3, 3, 128, 128], replicated
- grad_temporal: float32 [3, 128, 128], replicated
All inputs are finite; a program needn't handle non-finite values.
Results may differ from a plain program's by a relative error of at most 0.0032.
Values may be sent and summed in bfloat16 or wider, within the bound.
A program may use at most 64 MiB of HBM per device.

v0:
```python
import functools
import math

import jax
import jax.numpy as jnp
from jax import lax
from jax.experimental import pallas as pl
from jax.experimental.pallas import tpu as pltpu
from jax.sharding import PartitionSpec as P

MESH = pl.DeviceIdType.MESH
PAIR_WIRE = jnp.float32
PART_WIRE = jnp.bfloat16
SUM_WIRE = jnp.bfloat16
FIRST = 0
MOMENT = 2
LATE_OUT = False


def at(start, size):
    return pl.ds(pl.multiple_of(start, 16), size)


def each(count, act):
    def step(index, carry):
        act(index)
        return carry

    lax.fori_loop(1, count, step, 0)


def frames(first, last, act):
    def step(index, carry):
        act(index)
        return carry

    lax.fori_loop(first, last, step, 0)


def columns(rows, width, channels):
    place = lax.broadcasted_iota(jnp.int32, (rows // width, width, channels), 1)
    return place.reshape(rows, channels)


def before(value, place):
    return jnp.where(place == 0, 0.0, pltpu.roll(value, 1, 0))


def after(value, place, width):
    return jnp.where(place == width - 1, 0.0, pltpu.roll(value, value.shape[0] - 1, 0))


def spread(value, place, width):
    kind = jnp.bfloat16
    return jnp.concatenate(
        [after(value, place, width).astype(kind), value.astype(kind), before(value, place).astype(kind)],
        axis=1,
    )


def flat(value):
    return value.reshape(-1, value.shape[-1])


def across(left, right):
    return lax.dot_general(
        left, right, (((1,), (1,)), ((), ())), preferred_element_type=jnp.float32
    )


def contract(left, right):
    return lax.dot_general(
        left, right, (((0,), (0,)), ((), ())), preferred_element_type=jnp.float32
    )


def kernel(
    tiles,
    shards,
    scale,
    latent_ref,
    fwd_ref,
    rev_ref,
    space_ref,
    time_ref,
    out_f_ref,
    out_r_ref,
    grad_in_ref,
    grad_s_ref,
    grad_t_ref,
    cells,
    cot_f,
    cot_r,
    acts,
    pre,
    wide,
    rim_out,
    rim_in,
    space_fwd,
    space_back,
    time_back,
    sums,
    pair_out,
    pair_in,
    mid,
    mid_out,
    shard_in,
    total,
    out_f,
    out_r,
    grad_in,
    grad_s,
    grad_t,
    load_sem,
    store_sem,
    send_sem,
    recv_sem,
):
    tile, shard = lax.axis_index("tile"), lax.axis_index("tm")
    count, height, width, channels = latent_ref.shape
    plane = height * width
    taps = 3

    def tile_peer(step):
        return {"tile": lax.rem(tile + step, tiles)}

    def shard_peer(step):
        return {"tm": lax.rem(shard + step, shards)}

    barrier = pltpu.get_barrier_semaphore()

    def greet(peer):
        pl.semaphore_signal(barrier, inc=1, device_id=peer, device_id_type=MESH)

    each(tiles, lambda step: greet(tile_peer(step)))
    each(shards, lambda step: greet(shard_peer(step)))

    loads = [
        pltpu.make_async_copy(latent_ref, cells.at[:, pl.ds(1, height)], load_sem.at[0]),
        pltpu.make_async_copy(fwd_ref, cot_f.at[pl.ds(0, count)], load_sem.at[1]),
        pltpu.make_async_copy(rev_ref, cot_r.at[pl.ds(2, count)], load_sem.at[2]),
    ]
    for load in loads:
        load.start()

    has_next_tile, has_last_tile = tile < tiles - 1, tile > 0
    has_next_shard, has_last_shard = shard < shards - 1, shard > 0

    def remote(src, dst, index, peer):
        return pltpu.make_async_remote_copy(
            src_ref=src,
            dst_ref=dst,
            send_sem=send_sem.at[index],
            recv_sem=recv_sem.at[index],
            device_id=peer,
            device_id_type=MESH,
        )

    next_tile, last_tile = tile_peer(1), tile_peer(tiles - 1)
    next_shard, last_shard = shard_peer(1), shard_peer(shards - 1)
    up = (next_tile, has_next_tile, has_last_tile)
    down = (last_tile, has_last_tile, has_next_tile)
    later = (next_shard, has_next_shard, has_last_shard)
    earlier = (last_shard, has_last_shard, has_next_shard)
    moves = [
        (latent_ref.at[:, height - 1], cells.at[:, 0], *up),
        (latent_ref.at[:, 0], cells.at[:, height + 1], *down),
        (fwd_ref.at[0], cot_f.at[count], *earlier),
        (rev_ref.at[count - 1], cot_r.at[1], *later),
        (fwd_ref.at[1], cot_f.at[count + 1], *earlier),
        (rev_ref.at[count - 2], cot_r.at[0], *later),
        (acts.at[count + 1], acts.at[1], *later),
        (acts.at[2], acts.at[count + 2], *earlier),
        (acts.at[count], acts.at[0], *later),
        (acts.at[3], acts.at[count + 3], *earlier),
        (rim_out.at[1], rim_in.at[0], *up),
        (rim_out.at[0], rim_in.at[1], *down),
    ]
    copies = [remote(src, dst, index, peer) for index, (src, dst, peer, _, _) in enumerate(moves)]

    def launch(index):
        pl.when(moves[index][3])(copies[index].start)

    def arrive(index):
        pl.when(moves[index][4])(copies[index].wait_recv)

    def leave(index):
        pl.when(moves[index][3])(copies[index].wait_send)

    for index in range(len(moves)):
        target = moves[index][1]

        @pl.when(jnp.logical_not(moves[index][4]))
        def _(target=target):
            target[...] = jnp.zeros(target.shape, target.dtype)

    sums[...] = jnp.zeros_like(sums)
    for row in range(taps):
        time_back[:, row * channels : (row + 1) * channels] = time_ref[
            row * channels : (row + 1) * channels, :
        ]
        time_back[:, (taps + row) * channels : (taps + row + 1) * channels] = time_ref[
            row * channels : (row + 1) * channels, :
        ]
        for col in range(taps):
            index = row * taps + col
            weight = space_ref[index * channels : (index + 1) * channels, :]
            space_fwd[
                row * channels : (row + 1) * channels, col * channels : (col + 1) * channels
            ] = weight
            space_back[:, index * channels : (index + 1) * channels] = weight

    pl.semaphore_wait(barrier, tiles + shards - 2)
    for index in range(6):
        launch(index)
    place = columns(plane, width, channels)

    def window(frame):
        return jnp.concatenate(
            [flat(cells[frame, pl.ds(row, height)]) for row in range(taps)], axis=1
        )

    loads[0].wait()
    arrive(0)
    arrive(1)

    def convolve(frame):
        parts = jnp.dot(window(frame), space_fwd[...], preferred_element_type=jnp.float32)
        value = (
            before(parts[:, :channels], place)
            + parts[:, channels : 2 * channels]
            + after(parts[:, 2 * channels :], place, width)
        )
        pre[frame] = value
        act = value / (1.0 + jnp.exp(-value))
        acts[frame + 2] = act.astype(jnp.bfloat16).reshape(height, width, channels)

    frames(0, count, convolve)

    def second_acts(moment):
        if moment == FIRST:
            launch(6)
            launch(7)
        if moment == MOMENT:
            launch(8)
            launch(9)

    def backward(frame):
        joined = jnp.concatenate(
            [flat(cot_f[frame + lag]) for lag in range(taps)]
            + [flat(cot_r[frame + 2 - lag]) for lag in range(taps)],
            axis=1,
        )
        grad_act = across(joined, time_back[...])
        value = pre[frame]
        gate = 1.0 / (1.0 + jnp.exp(-value))
        grad = grad_act * gate * (1.0 + value * (1.0 - gate))
        grad = grad.astype(jnp.bfloat16).astype(jnp.float32)
        shifted = spread(grad, place, width)
        wide[frame, pl.ds(1, height)] = shifted.reshape(height, width, taps * channels)
        rounded = grad.astype(jnp.bfloat16)
        rim_out[0, frame] = rounded[:width]
        rim_out[1, frame] = rounded[plane - width :]
        lags = contract(flat(acts[frame + 2]), joined)
        for lag in range(taps):
            row = (taps * taps + lag) * channels
            sums[row : row + channels, :] += (
                lags[:, lag * channels : (lag + 1) * channels]
                + lags[:, (taps + lag) * channels : (taps + lag + 1) * channels]
            )
        part = contract(window(frame), shifted)
        for row in range(taps):
            for col in range(taps):
                start = (row * taps + col) * channels
                sums[start : start + channels, :] += part[
                    row * channels : (row + 1) * channels, col * channels : (col + 1) * channels
                ]

    loads[1].wait()
    loads[2].wait()
    arrive(2)
    arrive(3)
    frames(1, count - 1, backward)
    for index in (2, 3, 4, 5):
        leave(index)
    second_acts(0)
    arrive(4)
    arrive(5)
    backward(0)
    backward(count - 1)
    launch(10)
    launch(11)

    half = sums.shape[0] // tiles
    chunk = half // shards

    def settle(phase, ref):
        pltpu.make_async_copy(ref, ref, send_sem.at[phase]).wait()
        pltpu.make_async_copy(ref, ref, recv_sem.at[phase]).wait()

    def rows_to(step):
        return lax.rem(tile + step, tiles) * half

    pair_out[...] = sums[...].astype(PAIR_WIRE)
    each(
        tiles,
        lambda step: remote(
            pair_out.at[at(rows_to(step), half)], pair_in.at[step - 1], 12, tile_peer(step)
        ).start(),
    )

    second_acts(1)

    def outputs(frame):
        base = flat(cells[frame, pl.ds(1, height)]).astype(jnp.float32)
        causal = jnp.concatenate([flat(acts[frame + 2 - lag]) for lag in range(taps)], axis=1)
        anticausal = jnp.concatenate([flat(acts[frame + 2 + lag]) for lag in range(taps)], axis=1)
        for joined, ref in ((causal, out_f), (anticausal, out_r)):
            value = base + jnp.dot(joined, time_ref[...], preferred_element_type=jnp.float32)
            ref[frame] = value.astype(jnp.bfloat16).reshape(height, width, channels)

    def all_outputs():
        for index in range(6, 10):
            arrive(index)
        frames(0, count, outputs)
        stores[0].start()
        stores[1].start()

    def input_grads(frame):
        joined = jnp.concatenate(
            [flat(wide[frame, pl.ds(2 - row, height)]) for row in range(taps)], axis=1
        )
        value = flat(cot_f[frame]).astype(jnp.float32) + flat(cot_r[frame + 2]).astype(jnp.float32)
        value = value + across(joined, space_back[...])
        grad_in[frame] = value.astype(jnp.bfloat16).reshape(height, width, channels)

    stores = [
        pltpu.make_async_copy(src, dst, store_sem.at[index])
        for index, (src, dst) in enumerate(
            (
                (out_f, out_f_ref),
                (out_r, out_r_ref),
                (grad_in, grad_in_ref),
                (grad_s, grad_s_ref),
                (grad_t, grad_t_ref),
            )
        )
    ]
    settle(12, pair_in)
    own_half = sums[at(tile * half, half), :]
    for index in range(tiles - 1):
        own_half = own_half + pair_in[index].astype(jnp.float32)
    mid[...] = own_half
    mid_out[...] = own_half.astype(PART_WIRE)
    each(
        shards,
        lambda step: remote(
            mid_out.at[at(lax.rem(shard + step, shards) * chunk, chunk)],
            shard_in.at[step - 1],
            13,
            shard_peer(step),
        ).start(),
    )
    second_acts(2)
    settle(13, shard_in)
    part = lax.fori_loop(
        0,
        shards - 1,
        lambda index, value: value + shard_in[index].astype(jnp.float32),
        mid[at(shard * chunk, chunk), :],
    )
    own = at(tile * half + shard * chunk, chunk)
    total[own, :] = (part * scale).astype(SUM_WIRE)
    each(
        shards,
        lambda step: remote(total.at[own], total.at[own], 14, shard_peer(step)).start(),
    )
    second_acts(3)
    arrive(10)
    arrive(11)
    edge = columns(count * width, width, channels)
    for side, row in ((0, 0), (1, height + 1)):
        rim = spread(flat(rim_in[side]).astype(jnp.float32), edge, width)
        wide[:, row] = rim.reshape(count, width, taps * channels)
    frames(0, count, input_grads)
    stores[2].start()
    if not LATE_OUT:
        all_outputs()
    settle(14, total.at[pl.ds(0, (shards - 1) * chunk)])
    mine = at(tile * half, half)
    each(
        tiles,
        lambda step: remote(total.at[mine], total.at[mine], 15, tile_peer(step)).start(),
    )
    if LATE_OUT:
        all_outputs()
    for index in (0, 1, 6, 7, 8, 9, 10, 11):
        leave(index)
    settle(15, total.at[pl.ds(0, (tiles - 1) * half)])
    split = taps * taps * channels
    grad_s[...] = total[:split, :].astype(jnp.float32)
    stores[3].start()
    grad_t[...] = total[split : split + taps * channels, :].astype(jnp.float32)
    stores[4].start()
    for store in stores:
        store.wait()


def deliver_kernel(*refs):
    count = (len(refs) - 2) // 3
    sources, targets, held = refs[:count], refs[count : 2 * count], refs[2 * count : 3 * count]
    load_sem, store_sem = refs[3 * count :]
    loads, stores = [], []
    for index in range(count):
        loads.append(pltpu.make_async_copy(sources[index], held[index], load_sem.at[index]))
        stores.append(pltpu.make_async_copy(held[index], targets[index], store_sem.at[index]))
    for load in loads:
        load.start()
    for load, store in zip(loads, stores):
        load.wait()
        store.start()
    for store in stores:
        store.wait()


def deliver(*values):
    hbm = pl.BlockSpec(memory_space=pl.ANY)
    count = len(values)
    return pl.pallas_call(
        deliver_kernel,
        out_shape=tuple(jax.ShapeDtypeStruct(value.shape, value.dtype) for value in values),
        in_specs=[hbm] * count,
        out_specs=(hbm,) * count,
        scratch_shapes=[pltpu.VMEM(value.shape, value.dtype) for value in values]
        + [pltpu.SemaphoreType.DMA((count,)), pltpu.SemaphoreType.DMA((count,))],
    )(*values)


def body(latent, cot_forward, cot_reverse, spatial_weight, temporal_weight):
    tiles, shards = lax.axis_size("tile"), lax.axis_size("tm")
    count, height, width, channels = latent.shape
    positions = count * height * width * shards * tiles
    scale = 1.0 / math.sqrt(positions)
    rows = 12 * channels
    unit = 16 * tiles * shards
    padded = -(-rows // unit) * unit
    half = padded // tiles
    chunk = half // shards
    kind = jnp.bfloat16
    vmem = pl.BlockSpec(memory_space=pltpu.VMEM)
    hbm = pl.BlockSpec(memory_space=pl.ANY)
    results = pl.pallas_call(
        functools.partial(kernel, tiles, shards, scale),
        out_shape=(
            jax.ShapeDtypeStruct(latent.shape, kind),
            jax.ShapeDtypeStruct(latent.shape, kind),
            jax.ShapeDtypeStruct(latent.shape, kind),
            jax.ShapeDtypeStruct((9 * channels, channels), jnp.float32),
            jax.ShapeDtypeStruct((3 * channels, channels), jnp.float32),
        ),
        in_specs=[hbm, hbm, hbm, vmem, vmem],
        out_specs=(hbm, hbm, hbm, hbm, hbm),
        scratch_shapes=[
            pltpu.VMEM((count, height + 2, width, channels), kind),
            pltpu.VMEM((count + 2, height, width, channels), kind),
            pltpu.VMEM((count + 2, height, width, channels), kind),
            pltpu.VMEM((count + 4, height, width, channels), kind),
            pltpu.VMEM((count, height * width, channels), jnp.float32),
            pltpu.VMEM((count, height + 2, width, 3 * channels), kind),
            pltpu.VMEM((2, count, width, channels), kind),
            pltpu.VMEM((2, count, width, channels), kind),
            pltpu.VMEM((3 * channels, 3 * channels), kind),
            pltpu.VMEM((channels, 9 * channels), kind),
            pltpu.VMEM((channels, 6 * channels), kind),
            pltpu.VMEM((padded, channels), jnp.float32),
            pltpu.VMEM((padded, channels), PAIR_WIRE),
            pltpu.VMEM((tiles - 1, half, channels), PAIR_WIRE),
            pltpu.VMEM((half, channels), jnp.float32),
            pltpu.VMEM((half, channels), PART_WIRE),
            pltpu.VMEM((shards - 1, chunk, channels), PART_WIRE),
            pltpu.VMEM((padded, channels), SUM_WIRE),
            pltpu.VMEM(latent.shape, kind),
            pltpu.VMEM(latent.shape, kind),
            pltpu.VMEM(latent.shape, kind),
            pltpu.VMEM((9 * channels, channels), jnp.float32),
            pltpu.VMEM((3 * channels, channels), jnp.float32),
            pltpu.SemaphoreType.DMA((3,)),
            pltpu.SemaphoreType.DMA((5,)),
            pltpu.SemaphoreType.DMA((16,)),
            pltpu.SemaphoreType.DMA((16,)),
        ],
        compiler_params=pltpu.CompilerParams(collective_id=0, has_side_effects=True),
    )(
        latent,
        cot_forward,
        cot_reverse,
        spatial_weight.reshape(9 * channels, channels),
        temporal_weight.reshape(3 * channels, channels),
    )
    out_f, out_r, grad_in, grad_s, grad_t = deliver(*results)
    return (
        out_f,
        out_r,
        grad_in,
        grad_s.reshape(spatial_weight.shape),
        grad_t.reshape(temporal_weight.shape),
    )


def solution(mesh):
    placed = (
        P("tm", "tile", None, None),
        P("tm", "tile", None, None),
        P("tm", "tile", None, None),
        P(),
        P(),
    )
    return jax.shard_map(
        body,
        mesh=mesh,
        in_specs=placed,
        out_specs=(
            P("tm", "tile", None, None),
            P("tm", "tile", None, None),
            P("tm", "tile", None, None),
            P(),
            P(),
        ),
        check_vma=False,
    )
```

profile of v0, /device:TPU:0, one launch (start us, length us, event | category | flops | bytes accessed | tf_op | source)
XLA Modules:
  0.0 49.5 jit_solution(6812911555764266584)
XLA Ops:
  0.6 46.1 %shard_map.92 = (bf16[4,4,160,128]{3,2,1,0:T(8,128)(2,1)}, bf16[4,4,160,128]{3,2,1,0:T(8,128)(2,1)}, bf16[4,4,160,128]{3,2,1,0:T(8,128)(2,1)}, f32[1152,128]{1,0:T(8,128)}, f32[384,128]{1,0:T(8,128)}) custom-call(bf16[4,4,160,128]{3,2,1,0:T(8,128)(2,1)} %latent_ref.1, bf16[4,4,160,128]{3,2,1,0:T(8,128)(2,1)} %fwd_ref.1, bf16[4,4,160,128]{3,2,1,0:T(8,128)(2,1)} %rev_ref.1, ...), custom_call_target="tpu_custom_call" | custom-call | tf_op jit(solution)/shard_map/pallas_call | solution.py:452
  46.8 2.7 %shard_map.93 = (bf16[4,4,160,128]{3,2,1,0:T(8,128)(2,1)}, bf16[4,4,160,128]{3,2,1,0:T(8,128)(2,1)}, bf16[4,4,160,128]{3,2,1,0:T(8,128)(2,1)}, f32[1152,128]{1,0:T(8,128)}, f32[384,128]{1,0:T(8,128)}) custom-call(bf16[4,4,160,128]{3,2,1,0:T(8,128)(2,1)} %get-tuple-element.15.refs_0_, bf16[4,4,160,128]{3,2,1,0:T(8,128)(2,1)} %get-tuple-element.16.refs_1_, ...), custom_call_target="tpu_custom_call" | custom-call | tf_op jit(solution)/shard_map/pallas_call | solution.py:429
where the time goes:
time: 50.3 us; the launch traced here: 49.5 us
  Pallas kernels  48.8 us (97%)
  between operations  0.64 us (1%)
    pallas_call x1, Pallas kernels, body(): pl.pallas_call(functools.partial(kernel, tiles, shards, scale), out_shape...  46.1 us
    pallas_call x1, Pallas kernels, deliver(): pl.pallas_call(deliver_kernel, out_shape=tuple((jax.ShapeDtypeStruct(valu...  2.69 us

commit v1 on v0

--- a/solution.py
+++ b/solution.py
@@ -15,6 +15,7 @@
 FIRST = 0
 MOMENT = 2
 LATE_OUT = False
+VMEM_LIMIT = 32 << 20
 
 
 def at(start, size):
@@ -81,13 +82,13 @@
     latent_ref,
     fwd_ref,
     rev_ref,
-    space_ref,
-    time_ref,
-    out_f_ref,
-    out_r_ref,
-    grad_in_ref,
-    grad_s_ref,
-    grad_t_ref,
+    space_hbm,
+    time_hbm,
+    out_f,
+    out_r,
+    grad_in,
+    grad_s,
+    grad_t,
     cells,
     cot_f,
     cot_r,
@@ -106,13 +107,9 @@
     mid_out,
     shard_in,
     total,
-    out_f,
-    out_r,
-    grad_in,
-    grad_s,
-    grad_t,
+    space_ref,
+    time_ref,
     load_sem,
-    store_sem,
     send_sem,
     recv_sem,
 ):
@@ -139,6 +136,8 @@
         pltpu.make_async_copy(latent_ref, cells.at[:, pl.ds(1, height)], load_sem.at[0]),
         pltpu.make_async_copy(fwd_ref, cot_f.at[pl.ds(0, count)], load_sem.at[1]),
         pltpu.make_async_copy(rev_ref, cot_r.at[pl.ds(2, count)], load_sem.at[2]),
+        pltpu.make_async_copy(space_hbm, space_ref, load_sem.at[3]),
+        pltpu.make_async_copy(time_hbm, time_ref, load_sem.at[4]),
     ]
     for load in loads:
         load.start()
@@ -195,6 +194,8 @@
             target[...] = jnp.zeros(target.shape, target.dtype)
 
     sums[...] = jnp.zeros_like(sums)
+    loads[3].wait()
+    loads[4].wait()
     for row in range(taps):
         time_back[:, row * channels : (row + 1) * channels] = time_ref[
             row * channels : (row + 1) * channels, :
@@ -323,8 +324,6 @@
         for index in range(6, 10):
             arrive(index)
         frames(0, count, outputs)
-        stores[0].start()
-        stores[1].start()
 
     def input_grads(frame):
         joined = jnp.concatenate(
@@ -334,18 +333,6 @@
         value = value + across(joined, space_back[...])
         grad_in[frame] = value.astype(jnp.bfloat16).reshape(height, width, channels)
 
-    stores = [
-        pltpu.make_async_copy(src, dst, store_sem.at[index])
-        for index, (src, dst) in enumerate(
-            (
-                (out_f, out_f_ref),
-                (out_r, out_r_ref),
-                (grad_in, grad_in_ref),
-                (grad_s, grad_s_ref),
-                (grad_t, grad_t_ref),
-            )
-        )
-    ]
     settle(12, pair_in)
     own_half = sums[at(tile * half, half), :]
     for index in range(tiles - 1):
@@ -383,7 +370,6 @@
         rim = spread(flat(rim_in[side]).astype(jnp.float32), edge, width)
         wide[:, row] = rim.reshape(count, width, taps * channels)
     frames(0, count, input_grads)
-    stores[2].start()
     if not LATE_OUT:
         all_outputs()
     settle(14, total.at[pl.ds(0, (shards - 1) * chunk)])
@@ -399,25 +385,16 @@
     settle(15, total.at[pl.ds(0, (tiles - 1) * half)])
     split = taps * taps * channels
     grad_s[...] = total[:split, :].astype(jnp.float32)
-    stores[3].start()
     grad_t[...] = total[split : split + taps * channels, :].astype(jnp.float32)
-    stores[4].start()
+
+
+def deliver_kernel(*refs):
+    count = (len(refs) - 1) // 2
+    stores = [
+        pltpu.make_async_copy(refs[index], refs[count + index], refs[-1].at[index])
+        for index in range(count)
+    ]
     for store in stores:
-        store.wait()
-
-
-def deliver_kernel(*refs):
-    count = (len(refs) - 2) // 3
-    sources, targets, held = refs[:count], refs[count : 2 * count], refs[2 * count : 3 * count]
-    load_sem, store_sem = refs[3 * count :]
-    loads, stores = [], []
-    for index in range(count):
-        loads.append(pltpu.make_async_copy(sources[index], held[index], load_sem.at[index]))
-        stores.append(pltpu.make_async_copy(held[index], targets[index], store_sem.at[index]))
-    for load in loads:
-        load.start()
-    for load, store in zip(loads, stores):
-        load.wait()
         store.start()
     for store in stores:
         store.wait()
@@ -425,15 +402,16 @@
 
 def deliver(*values):
     hbm = pl.BlockSpec(memory_space=pl.ANY)
+    vmem = pl.BlockSpec(memory_space=pltpu.VMEM)
     count = len(values)
     return pl.pallas_call(
         deliver_kernel,
         out_shape=tuple(jax.ShapeDtypeStruct(value.shape, value.dtype) for value in values),
-        in_specs=[hbm] * count,
+        in_specs=[vmem] * count,
         out_specs=(hbm,) * count,
-        scratch_shapes=[pltpu.VMEM(value.shape, value.dtype) for value in values]
-        + [pltpu.SemaphoreType.DMA((count,)), pltpu.SemaphoreType.DMA((count,))],
-    )(*values)
+        scratch_shapes=[pltpu.SemaphoreType.DMA((count,))],
+        compiler_params=pltpu.CompilerParams(vmem_limit_bytes=VMEM_LIMIT),
+    )(*(pltpu.with_memory_space_constraint(value, pltpu.VMEM) for value in values))
 
 
 def body(latent, cot_forward, cot_reverse, spatial_weight, temporal_weight):
@@ -448,18 +426,18 @@
     chunk = half // shards
     kind = jnp.bfloat16
     vmem = pl.BlockSpec(memory_space=pltpu.VMEM)
-    hbm = pl.BlockSpec(memory_space=pl.ANY)
+    hbm = pl.BlockSpec(memory_space=pltpu.HBM)
     results = pl.pallas_call(
         functools.partial(kernel, tiles, shards, scale),
         out_shape=(
-            jax.ShapeDtypeStruct(latent.shape, kind),
-            jax.ShapeDtypeStruct(latent.shape, kind),
-            jax.ShapeDtypeStruct(latent.shape, kind),
-            jax.ShapeDtypeStruct((9 * channels, channels), jnp.float32),
-            jax.ShapeDtypeStruct((3 * channels, channels), jnp.float32),
+            pltpu.VMEM(latent.shape, kind),
+            pltpu.VMEM(latent.shape, kind),
+            pltpu.VMEM(latent.shape, kind),
+            pltpu.VMEM((9 * channels, channels), jnp.float32),
+            pltpu.VMEM((3 * channels, channels), jnp.float32),
         ),
-        in_specs=[hbm, hbm, hbm, vmem, vmem],
-        out_specs=(hbm, hbm, hbm, hbm, hbm),
+        in_specs=[hbm] * 5,
+        out_specs=(vmem,) * 5,
         scratch_shapes=[
             pltpu.VMEM((count, height + 2, width, channels), kind),
             pltpu.VMEM((count + 2, height, width, channels), kind),
@@ -479,23 +457,24 @@
             pltpu.VMEM((half, channels), PART_WIRE),
             pltpu.VMEM((shards - 1, chunk, channels), PART_WIRE),
             pltpu.VMEM((padded, channels), SUM_WIRE),
-            pltpu.VMEM(latent.shape, kind),
-            pltpu.VMEM(latent.shape, kind),
-            pltpu.VMEM(latent.shape, kind),
-            pltpu.VMEM((9 * channels, channels), jnp.float32),
-            pltpu.VMEM((3 * channels, channels), jnp.float32),
-            pltpu.SemaphoreType.DMA((3,)),
+            pltpu.VMEM((9 * channels, channels), kind),
+            pltpu.VMEM((3 * channels, channels), kind),
             pltpu.SemaphoreType.DMA((5,)),
             pltpu.SemaphoreType.DMA((16,)),
             pltpu.SemaphoreType.DMA((16,)),
         ],
-        compiler_params=pltpu.CompilerParams(collective_id=0, has_side_effects=True),
+        compiler_params=pltpu.CompilerParams(collective_id=0, has_side_effects=True, vmem_limit_bytes=VMEM_LIMIT),
     )(
-        latent,
-        cot_forward,
-        cot_reverse,
-        spatial_weight.reshape(9 * channels, channels),
-        temporal_weight.reshape(3 * channels, channels),
+        *(
+            pltpu.with_memory_space_constraint(value, pltpu.HBM)
+            for value in (
+                latent,
+                cot_forward,
+                cot_reverse,
+                spatial_weight.reshape(9 * channels, channels),
+                temporal_weight.reshape(3 * channels, channels),
+            )
+        ),
     )
     out_f, out_r, grad_in, grad_s, grad_t = deliver(*results)
     return (

time: 50.3 us -> 47.4 us (0.942)
  the two profiles are of different devices: /device:TPU:0 before, /device:TPU:17 now
where the time goes in v1:
time: 47.4 us; the launch traced here: 47.3 us
  Pallas kernels  46.6 us (98%)
  between operations  0.64 us (1%)
    pallas_call x1, Pallas kernels, body(): pl.pallas_call(functools.partial(kernel, tiles, shards, scale), out_shape...  45.1 us
    pallas_call x1, Pallas kernels, deliver(): pl.pallas_call(deliver_kernel, out_shape=tuple((jax.ShapeDtypeStruct(valu...  1.56 us

profile of v1, /device:TPU:17, one launch (start us, length us, event | category | flops | bytes accessed | tf_op | source)
XLA Modules:
  0.0 47.3 jit_solution(9522960706263100138)
XLA Ops:
  0.6 45.1 %shard_map.92 = (bf16[4,4,160,128]{3,2,1,0:T(8,128)(2,1)S(1)}, bf16[4,4,160,128]{3,2,1,0:T(8,128)(2,1)S(1)}, bf16[4,4,160,128]{3,2,1,0:T(8,128)(2,1)S(1)}, f32[1152,128]{1,0:T(8,128)S(1)}, f32[384,128]{1,0:T(8,128)S(1)}) custom-call(bf16[4,4,160,128]{3,2,1,0:T(8,128)(2,1)} %latent_ref.1, bf16[4,4,160,128]{3,2,1,0:T(8,128)(2,1)} %fwd_ref.1, ...), custom_call_target="tpu_custom_call" | custom-call | tf_op jit(solution)/shard_map/pallas_call | solution.py:430
  45.7 1.6 %shard_map.93 = (bf16[4,4,160,128]{3,2,1,0:T(8,128)(2,1)}, bf16[4,4,160,128]{3,2,1,0:T(8,128)(2,1)}, bf16[4,4,160,128]{3,2,1,0:T(8,128)(2,1)}, f32[1152,128]{1,0:T(8,128)}, f32[384,128]{1,0:T(8,128)}) custom-call(bf16[4,4,160,128]{3,2,1,0:T(8,128)(2,1)S(1)} %get-tuple-element.15.refs_0_, bf16[4,4,160,128]{3,2,1,0:T(8,128)(2,1)S(1)} %get-tuple-element.16.refs_1_, ...), custom_call_target="tpu_custom_call" | custom-call | tf_op jit(solution)/shard_map/pallas_call | solution.py:407

commit v2 on v1

v2 whole, which is shorter than its diff:
```python
import functools
import math

import jax
import jax.numpy as jnp
from jax import lax
from jax.experimental import pallas as pl
from jax.experimental.pallas import tpu as pltpu
from jax.sharding import PartitionSpec as P

MESH = pl.DeviceIdType.MESH
KIND = jnp.bfloat16
TAPS = 3
REACH = TAPS - 1
PIECES = 2
PARTS = 2
ACTS_AT = (4, 6, 8)
VMEM_LIMIT = 32 << 20


def at(start, size):
    return pl.ds(pl.multiple_of(start, 16), size)


def each(count, act):
    def step(index, carry):
        act(index)
        return carry

    lax.fori_loop(1, count, step, 0)


def frames(first, last, act):
    def step(index, carry):
        act(index)
        return carry

    lax.fori_loop(first, last, step, 0)


def columns(rows, width, channels):
    place = lax.broadcasted_iota(jnp.int32, (rows // width, width, channels), 1)
    return place.reshape(rows, channels)


def before(value, place):
    return jnp.where(place == 0, 0.0, pltpu.roll(value, 1, 0))


def after(value, place, width):
    return jnp.where(place == width - 1, 0.0, pltpu.roll(value, value.shape[0] - 1, 0))


def spread(value, place, width):
    return jnp.concatenate(
        [after(value, place, width).astype(KIND), value.astype(KIND), before(value, place).astype(KIND)],
        axis=1,
    )


def flat(value):
    return value.reshape(-1, value.shape[-1])


def across(left, right):
    return lax.dot_general(
        left, right, (((1,), (1,)), ((), ())), preferred_element_type=jnp.float32
    )


def contract(left, right):
    return lax.dot_general(
        left, right, (((0,), (0,)), ((), ())), preferred_element_type=jnp.float32
    )


def kernel(
    tiles,
    shards,
    scale,
    latent_ref,
    fwd_ref,
    rev_ref,
    space_hbm,
    time_hbm,
    out_f,
    out_r,
    grad_in,
    grad_s,
    grad_t,
    cells,
    cot_f,
    cot_r,
    acts,
    gates,
    pulls,
    wide,
    rim_out,
    rim_in,
    space_ref,
    time_ref,
    space_fwd,
    space_back,
    time_back,
    sums,
    pair_in,
    mid,
    mid_out,
    shard_in,
    mate_out,
    mate_in,
    total,
    load_sem,
    ready,
    halo_send,
    halo_recv,
    sum_send,
    sum_recv,
):
    tile, shard = lax.axis_index("tile"), lax.axis_index("tm")
    count, height, width, channels = latent_ref.shape
    plane = height * width
    mates = 2 if shards % 2 == 0 else 1
    crew = shards // mates

    def tile_peer(step):
        return {"tile": lax.rem(tile + step, tiles)}

    def shard_peer(step):
        return {"tm": lax.rem(shard + step, shards)}

    def crew_peer(step):
        return {"tm": lax.rem(shard + step * mates, shards)}

    def signal(semaphore, peer):
        pl.semaphore_signal(semaphore, inc=1, device_id=peer, device_id_type=MESH)

    loads = [
        pltpu.make_async_copy(src, dst, load_sem.at[index])
        for index, (src, dst) in enumerate(
            (
                (space_hbm, space_ref),
                (time_hbm, time_ref),
                (latent_ref, cells.at[:, pl.ds(1, height)]),
                (fwd_ref, cot_f.at[pl.ds(0, count)]),
                (rev_ref, cot_r.at[pl.ds(REACH, count)]),
            )
        )
    ]
    barrier = pltpu.get_barrier_semaphore()
    signal(barrier, shard_peer(1))
    signal(barrier, shard_peer(shards - 1))
    each(tiles, lambda step: signal(barrier, tile_peer(step)))
    for load in loads:
        load.start()

    has_next_tile, has_last_tile = tile < tiles - 1, tile > 0
    has_next_shard, has_last_shard = shard < shards - 1, shard > 0

    next_tile, last_tile = tile_peer(1), tile_peer(tiles - 1)
    next_shard, last_shard = shard_peer(1), shard_peer(shards - 1)
    up = (next_tile, has_next_tile, has_last_tile)
    down = (last_tile, has_last_tile, has_next_tile)
    later = (next_shard, has_next_shard, has_last_shard)
    earlier = (last_shard, has_last_shard, has_next_shard)
    moves = []

    def move(src, dst, way):
        moves.append((src, dst, *way))
        return len(moves) - 1

    cell_moves = [
        move(latent_ref.at[:, height - 1], cells.at[:, 0], up),
        move(latent_ref.at[:, 0], cells.at[:, height + 1], down),
    ]
    cot_moves = []
    for reach in range(REACH):
        cot_moves.append(
            [
                move(fwd_ref.at[reach], cot_f.at[count + reach], earlier),
                move(rev_ref.at[count - 1 - reach], cot_r.at[REACH - 1 - reach], later),
            ]
        )
    rim_moves = [move(rim_out.at[1], rim_in.at[0], up), move(rim_out.at[0], rim_in.at[1], down)]
    parts = PARTS if height % PARTS == 0 else 1
    rows = height // parts
    act_moves = []
    for reach in range(REACH):
        group = []
        for part in range(parts):
            cut = pl.ds(part * rows, rows)
            group.append(
                move(acts.at[count + 1 - reach, cut], acts.at[1 - reach, cut], later)
            )
            group.append(
                move(acts.at[REACH + reach, cut], acts.at[count + REACH + reach, cut], earlier)
            )
        act_moves.append(group)
    act_order = [index for group in act_moves for index in group]

    def remote(src, dst, send, recv, peer):
        return pltpu.make_async_remote_copy(
            src_ref=src, dst_ref=dst, send_sem=send, recv_sem=recv, device_id=peer, device_id_type=MESH
        )

    copies = [
        remote(src, dst, halo_send.at[index], halo_recv.at[index], peer)
        for index, (src, dst, peer, _, _) in enumerate(moves)
    ]

    def launch(indices):
        for index in indices:
            pl.when(moves[index][3])(copies[index].start)

    def arrive(indices):
        for index in indices:
            pl.when(moves[index][4])(copies[index].wait_recv)

    def leave(indices):
        for index in indices:
            pl.when(moves[index][3])(copies[index].wait_send)

    pl.semaphore_wait(barrier, tiles + 1)
    for group in cot_moves:
        launch(group)
    launch(cell_moves)
    spans = []
    span = 1
    while span * 2 < shards:
        spans.append(span)
        span *= 2

    def tell(index):
        signal(ready.at[index], shard_peer(spans[index]))
        signal(ready.at[index], shard_peer(shards - spans[index]))

    def hear(index):
        pl.semaphore_wait(ready.at[index], 2)

    tell(0)
    for index in range(len(moves)):
        target = moves[index][1]

        @pl.when(jnp.logical_not(moves[index][4]))
        def _(target=target):
            target[...] = jnp.zeros(target.shape, target.dtype)

    sums[...] = jnp.zeros_like(sums)
    place = columns(plane, width, channels)
    loads[0].wait()
    loads[1].wait()

    def block(index):
        return slice(index * channels, (index + 1) * channels)

    for row in range(TAPS):
        weight = time_ref[block(row), :]
        time_back[:, block(REACH - row)] = weight
        time_back[:, block(TAPS + row)] = weight
        for col in range(TAPS):
            weight = space_ref[block(row * TAPS + col), :]
            space_fwd[block(row), block(col)] = weight
            space_back[:, block(row * TAPS + col)] = weight

    def window(frame):
        return jnp.concatenate(
            [flat(cells[frame, pl.ds(row, height)]) for row in range(TAPS)], axis=1
        )

    loads[2].wait()
    arrive(cell_moves)

    def convolve(frame):
        taken = jnp.dot(window(frame), space_fwd[...], preferred_element_type=jnp.float32)
        value = (
            before(taken[:, :channels], place)
            + taken[:, channels : 2 * channels]
            + after(taken[:, 2 * channels :], place, width)
        )
        share = 1.0 / (1.0 + jnp.exp(-value))
        gates[frame] = share * (1.0 + value * (1.0 - share))
        act = value * share
        acts[frame + REACH] = act.astype(KIND).reshape(height, width, channels)

    frames(0, count, convolve)
    hear(0)
    for index in range(1, len(spans)):
        if index == 1:
            tell(1)
    sent = [0]

    def send_acts(moment):
        upto = min(ACTS_AT[moment] * len(act_order) // 8, len(act_order))
        launch(act_order[sent[0] : upto])
        sent[0] = upto

    send_acts(0)

    def add_lag(lag, value):
        sums[0, block(lag), :] += value

    def own_pull(frame):
        low = max(0, frame + REACH - (count - 1))
        high = min(REACH, frame)
        fwd = [flat(cot_f[frame + lag]) for lag in range(REACH - low, -1, -1)]
        rev = [flat(cot_r[frame + REACH - lag]) for lag in range(high + 1)]
        joined = jnp.concatenate(fwd + rev, axis=1)
        columns_of = slice(low * channels, (TAPS + high + 1) * channels)
        pulls[frame] = across(joined, time_back[:, columns_of])
        lags = contract(flat(acts[frame + REACH]), joined)
        for index in range(len(fwd)):
            add_lag(REACH - low - index, lags[:, block(index)])
        for lag in range(high + 1):
            add_lag(lag, lags[:, block(len(fwd) + lag)])

    loads[3].wait()
    loads[4].wait()
    for frame in range(count):
        own_pull(frame)
    for index in range(1, len(spans)):
        hear(index)
        if index + 1 < len(spans):
            tell(index + 1)

    def stage_of(frame):
        return max(0, REACH - frame, REACH - (count - 1 - frame))

    def halo_terms(frame, reach):
        terms = []
        lag = frame + reach
        if lag <= REACH:
            terms.append((lag, cot_r, REACH - reach))
        lag = count - 1 - frame + reach
        if lag <= REACH:
            terms.append((lag, cot_f, count + reach - 1))
        return terms

    def pull_halo(frame, reach):
        for lag, source, index in halo_terms(frame, reach):
            taken = flat(source[index])
            pulls[frame] += across(taken, time_back[:, block(TAPS + lag)])
            add_lag(lag, contract(flat(acts[frame + REACH]), taken))

    def settle_frame(frame):
        grad = (pulls[frame] * gates[frame]).astype(KIND)
        shifted = spread(grad.astype(jnp.float32), place, width)
        wide[frame, pl.ds(1, height)] = shifted.reshape(height, width, TAPS * channels)
        rim_out[0, frame] = grad[:width]
        rim_out[1, frame] = grad[plane - width :]
        part = contract(window(frame), shifted)
        for row in range(TAPS):
            for col in range(TAPS):
                tap = TAPS + row * TAPS + col
                spot = block(tap % (4 * TAPS // PIECES))
                sums[tap // (4 * TAPS // PIECES), spot, :] += part[block(row), block(col)]

    for frame in range(count):
        if stage_of(frame) == 0:
            settle_frame(frame)
    for reach in range(1, REACH + 1):
        arrive(cot_moves[reach - 1])
        for frame in range(count):
            if stage_of(frame) >= reach:
                pull_halo(frame, reach)
                if stage_of(frame) == reach:
                    settle_frame(frame)

    half = sums.shape[1] // tiles
    chunk = half // crew
    rank = shard // mates

    def settle(phase, piece, ref):
        spot = phase * PIECES + piece
        pltpu.make_async_copy(ref, ref, sum_send.at[spot]).wait()
        pltpu.make_async_copy(ref, ref, sum_recv.at[spot]).wait()

    def pass_on(phase, piece, src, dst, peer):
        spot = phase * PIECES + piece
        remote(src, dst, sum_send.at[spot], sum_recv.at[spot], peer).start()

    mine = at(tile * half, half)
    own = at(tile * half + rank * chunk, chunk)

    for piece in range(PIECES):
        each(
            tiles,
            lambda step, piece=piece: pass_on(
                0,
                piece,
                sums.at[piece, at(lax.rem(tile + step, tiles) * half, half)],
                pair_in.at[piece, step - 1],
                tile_peer(step),
            ),
        )
    launch(rim_moves)

    def out_forward(frame):
        joined = jnp.concatenate([flat(acts[frame + REACH - lag]) for lag in range(TAPS)], axis=1)
        value = flat(cells[frame, pl.ds(1, height)]).astype(jnp.float32)
        value = value + jnp.dot(joined, time_ref[...], preferred_element_type=jnp.float32)
        out_f[frame] = value.astype(KIND).reshape(height, width, channels)

    def out_reverse(frame):
        joined = jnp.concatenate([flat(acts[frame + REACH + lag]) for lag in range(TAPS)], axis=1)
        value = flat(cells[frame, pl.ds(1, height)]).astype(jnp.float32)
        value = value + jnp.dot(joined, time_ref[...], preferred_element_type=jnp.float32)
        out_r[frame] = value.astype(KIND).reshape(height, width, channels)

    def outputs(reach):
        for frame in range(count):
            if max(0, REACH - frame) == reach:
                out_forward(frame)
            if max(0, REACH - (count - 1 - frame)) == reach:
                out_reverse(frame)

    outputs(0)

    def scatter(piece):
        settle(0, piece, pair_in.at[piece])
        value = sums[piece, mine, :]
        for index in range(tiles - 1):
            value = value + pair_in[piece, index]
        mid[piece] = value
        mid_out[piece] = value.astype(KIND)
        each(
            crew,
            lambda step: pass_on(
                1,
                piece,
                mid_out.at[piece, at(lax.rem(rank + step, crew) * chunk, chunk)],
                shard_in.at[piece, step - 1],
                crew_peer(step),
            ),
        )

    for piece in range(PIECES):
        scatter(piece)
    send_acts(1)

    arrive(rim_moves)
    edge = columns(count * width, width, channels)
    for side, row in ((0, 0), (1, height + 1)):
        rim = spread(flat(rim_in[side]).astype(jnp.float32), edge, width)
        wide[:, row] = rim.reshape(count, width, TAPS * channels)

    def input_grads(frame):
        joined = jnp.concatenate(
            [flat(wide[frame, pl.ds(2 - row, height)]) for row in range(TAPS)], axis=1
        )
        value = flat(cot_f[frame]).astype(jnp.float32) + flat(cot_r[frame + REACH]).astype(jnp.float32)
        value = value + across(joined, space_back[...])
        grad_in[frame] = value.astype(KIND).reshape(height, width, channels)

    frames(0, count, input_grads)

    def share_mates(piece):
        settle(1, piece, shard_in.at[piece])
        value = lax.fori_loop(
            0,
            crew - 1,
            lambda index, value: value + shard_in[piece, index].astype(jnp.float32),
            mid[piece, at(rank * chunk, chunk), :],
        )
        mate_out[piece] = value
        if mates == 2:
            pass_on(
                2,
                piece,
                mate_out.at[piece],
                mate_in.at[piece],
                {"tm": shard + 1 - 2 * lax.rem(shard, 2)},
            )

    for piece in range(PIECES):
        share_mates(piece)
    send_acts(2)

    def gather(piece):
        value = mate_out[piece]
        if mates == 2:
            settle(2, piece, mate_in.at[piece])
            value = value + mate_in[piece]
        total[piece, own, :] = (value * scale).astype(KIND)
        each(
            crew,
            lambda step: pass_on(
                3, piece, total.at[piece, own], total.at[piece, own], crew_peer(step)
            ),
        )

    for piece in range(PIECES):
        gather(piece)

    arrive(act_moves[0])
    outputs(1)

    def forward_piece(piece):
        settle(3, piece, total.at[piece, pl.ds(0, (crew - 1) * chunk)])
        each(
            tiles,
            lambda step: pass_on(
                4, piece, total.at[piece, mine], total.at[piece, mine], tile_peer(step)
            ),
        )

    for piece in range(PIECES):
        forward_piece(piece)
    for reach in range(1, REACH):
        arrive(act_moves[reach])
        outputs(reach + 1)
    for piece in range(PIECES):
        settle(4, piece, total.at[piece, pl.ds(0, (tiles - 1) * half)])
    for tap in range(4 * TAPS):
        value = total[tap // (4 * TAPS // PIECES), block(tap % (4 * TAPS // PIECES)), :].astype(jnp.float32)
        if tap < TAPS:
            grad_t[block(tap), :] = value
        else:
            grad_s[block(tap - TAPS), :] = value
    leave(range(len(moves)))


def deliver_kernel(*refs):
    count = (len(refs) - 1) // 2
    stores = [
        pltpu.make_async_copy(refs[index], refs[count + index], refs[-1].at[index])
        for index in range(count)
    ]
    for store in stores:
        store.start()
    for store in stores:
        store.wait()


def deliver(*values):
    hbm = pl.BlockSpec(memory_space=pl.ANY)
    vmem = pl.BlockSpec(memory_space=pltpu.VMEM)
    count = len(values)
    return pl.pallas_call(
        deliver_kernel,
        out_shape=tuple(jax.ShapeDtypeStruct(value.shape, value.dtype) for value in values),
        in_specs=[vmem] * count,
        out_specs=(hbm,) * count,
        scratch_shapes=[pltpu.SemaphoreType.DMA((count,))],
        compiler_params=pltpu.CompilerParams(vmem_limit_bytes=VMEM_LIMIT),
    )(*(pltpu.with_memory_space_constraint(value, pltpu.VMEM) for value in values))


def body(latent, cot_forward, cot_reverse, spatial_weight, temporal_weight):
    tiles, shards = lax.axis_size("tile"), lax.axis_size("tm")
    count, height, width, channels = latent.shape
    positions = count * height * width * shards * tiles
    scale = 1.0 / math.sqrt(positions)
    mates = 2 if shards % 2 == 0 else 1
    crew = shards // mates
    rows = 4 * TAPS * channels // PIECES
    unit = 16 * tiles * crew
    padded = -(-rows // unit) * unit
    half = padded // tiles
    chunk = half // crew
    stages = max(1, (shards - 1).bit_length() - 1)
    parts = PARTS if height % PARTS == 0 else 1
    moves = 4 + REACH * 2 + REACH * 2 * parts
    vmem = pl.BlockSpec(memory_space=pltpu.VMEM)
    hbm = pl.BlockSpec(memory_space=pltpu.HBM)
    results = pl.pallas_call(
        functools.partial(kernel, tiles, shards, scale),
        out_shape=(
            pltpu.VMEM(latent.shape, KIND),
            pltpu.VMEM(latent.shape, KIND),
            pltpu.VMEM(latent.shape, KIND),
            pltpu.VMEM((9 * channels, channels), jnp.float32),
            pltpu.VMEM((3 * channels, channels), jnp.float32),
        ),
        in_specs=[hbm] * 5,
        out_specs=(vmem,) * 5,
        scratch_shapes=[
            pltpu.VMEM((count, height + 2, width, channels), KIND),
            pltpu.VMEM((count + REACH, height, width, channels), KIND),
            pltpu.VMEM((count + REACH, height, width, channels), KIND),
            pltpu.VMEM((count + 2 * REACH, height, width, channels), KIND),
            pltpu.VMEM((count, height * width, channels), jnp.float32),
            pltpu.VMEM((count, height * width, channels), jnp.float32),
            pltpu.VMEM((count, height + 2, width, TAPS * channels), KIND),
            pltpu.VMEM((2, count, width, channels), KIND),
            pltpu.VMEM((2, count, width, channels), KIND),
            pltpu.VMEM((9 * channels, channels), KIND),
            pltpu.VMEM((3 * channels, channels), KIND),
            pltpu.VMEM((3 * channels, 3 * channels), KIND),
            pltpu.VMEM((channels, 9 * channels), KIND),
            pltpu.VMEM((channels, 6 * channels), KIND),
            pltpu.VMEM((PIECES, padded, channels), jnp.float32),
            pltpu.VMEM((PIECES, tiles - 1, half, channels), jnp.float32),
            pltpu.VMEM((PIECES, half, channels), jnp.float32),
            pltpu.VMEM((PIECES, half, channels), KIND),
            pltpu.VMEM((PIECES, crew - 1, chunk, channels), KIND),
            pltpu.VMEM((PIECES, chunk, channels), jnp.float32),
            pltpu.VMEM((PIECES, chunk, channels), jnp.float32),
            pltpu.VMEM((PIECES, padded, channels), KIND),
            pltpu.SemaphoreType.DMA((5,)),
            pltpu.SemaphoreType.REGULAR((stages,)),
            pltpu.SemaphoreType.DMA((moves,)),
            pltpu.SemaphoreType.DMA((moves,)),
            pltpu.SemaphoreType.DMA((5 * PIECES,)),
            pltpu.SemaphoreType.DMA((5 * PIECES,)),
        ],
        compiler_params=pltpu.CompilerParams(
            collective_id=0, has_side_effects=True, vmem_limit_bytes=VMEM_LIMIT
        ),
    )(
        *(
            pltpu.with_memory_space_constraint(value, pltpu.HBM)
            for value in (
                latent,
                cot_forward,
                cot_reverse,
                spatial_weight.reshape(9 * channels, channels),
                temporal_weight.reshape(3 * channels, channels),
            )
        ),
    )
    out_f, out_r, grad_in, grad_s, grad_t = deliver(*results)
    return (
        out_f,
        out_r,
        grad_in,
        grad_s.reshape(spatial_weight.shape),
        grad_t.reshape(temporal_weight.shape),
    )


def solution(mesh):
    split, copied = P("tm", "tile", None, None), P()
    return jax.shard_map(
        body,
        mesh=mesh,
        in_specs=(split, split, split, copied, copied),
        out_specs=(split, split, split, copied, copied),
        check_vma=False,
    )
```

time: 47.4 us -> 46.2 us (0.975)
  the two profiles are of different devices: /device:TPU:17 before, /device:TPU:0 now
where the time goes in v2:
time: 46.2 us; the launch traced here: 46.1 us
  Pallas kernels  45.4 us (98%)
  between operations  0.64 us (1%)
    pallas_call x1, Pallas kernels, body(): pl.pallas_call(functools.partial(kernel, tiles, shards, scale), out_shape...  43.9 us
    pallas_call x1, Pallas kernels, deliver(): pl.pallas_call(deliver_kernel, out_shape=tuple((jax.ShapeDtypeStruct(valu...  1.56 us

profile of v2, /device:TPU:0, one launch (start us, length us, event | category | flops | bytes accessed | tf_op | source)
XLA Modules:
  0.0 46.1 jit_solution(16445900027388576953)
XLA Ops:
  0.6 43.9 %shard_map.92 = (bf16[4,4,160,128]{3,2,1,0:T(8,128)(2,1)S(1)}, bf16[4,4,160,128]{3,2,1,0:T(8,128)(2,1)S(1)}, bf16[4,4,160,128]{3,2,1,0:T(8,128)(2,1)S(1)}, f32[1152,128]{1,0:T(8,128)S(1)}, f32[384,128]{1,0:T(8,128)S(1)}) custom-call(bf16[4,4,160,128]{3,2,1,0:T(8,128)(2,1)} %latent_ref.1, bf16[4,4,160,128]{3,2,1,0:T(8,128)(2,1)} %fwd_ref.1, ...), custom_call_target="tpu_custom_call" | custom-call | tf_op jit(solution)/shard_map/pallas_call | solution.py:565
  44.5 1.6 %shard_map.93 = (bf16[4,4,160,128]{3,2,1,0:T(8,128)(2,1)}, bf16[4,4,160,128]{3,2,1,0:T(8,128)(2,1)}, bf16[4,4,160,128]{3,2,1,0:T(8,128)(2,1)}, f32[1152,128]{1,0:T(8,128)}, f32[384,128]{1,0:T(8,128)}) custom-call(bf16[4,4,160,128]{3,2,1,0:T(8,128)(2,1)S(1)} %get-tuple-element.15.refs_0_, bf16[4,4,160,128]{3,2,1,0:T(8,128)(2,1)S(1)} %get-tuple-element.16.refs_1_, ...), custom_call_target="tpu_custom_call" | custom-call | tf_op jit(solution)/shard_map/pallas_call | solution.py:538

commit v3 on v2

--- a/solution.py
+++ b/solution.py
@@ -12,9 +12,12 @@
 KIND = jnp.bfloat16
 TAPS = 3
 REACH = TAPS - 1
-PIECES = 2
+PIECES = 1
 PARTS = 2
-ACTS_AT = (4, 6, 8)
+MATES = 1
+HOLD = 1
+ACTS_AT = (0,0,4,4,8,8,12,16)
+ACTS_IN = (0,4,4,4,10,10,12,16)
 VMEM_LIMIT = 32 << 20
 
 
@@ -120,7 +123,7 @@
     tile, shard = lax.axis_index("tile"), lax.axis_index("tm")
     count, height, width, channels = latent_ref.shape
     plane = height * width
-    mates = 2 if shards % 2 == 0 else 1
+    mates = MATES if shards % MATES == 0 else 1
     crew = shards // mates
 
     def tile_peer(step):
@@ -148,14 +151,20 @@
         )
     ]
     barrier = pltpu.get_barrier_semaphore()
-    signal(barrier, shard_peer(1))
-    signal(barrier, shard_peer(shards - 1))
+    has_next_tile, has_last_tile = tile < tiles - 1, tile > 0
+    has_next_shard, has_last_shard = shard < shards - 1, shard > 0
+
+    def around(semaphore, span):
+        pl.when(shard + span < shards)(lambda: signal(semaphore, {"tm": shard + span}))
+        pl.when(shard >= span)(lambda: signal(semaphore, {"tm": shard - span}))
+
+    def near(span):
+        return (shard + span < shards).astype(jnp.int32) + (shard >= span).astype(jnp.int32)
+
+    around(barrier, 1)
     each(tiles, lambda step: signal(barrier, tile_peer(step)))
     for load in loads:
         load.start()
-
-    has_next_tile, has_last_tile = tile < tiles - 1, tile > 0
-    has_next_shard, has_last_shard = shard < shards - 1, shard > 0
 
     next_tile, last_tile = tile_peer(1), tile_peer(tiles - 1)
     next_shard, last_shard = shard_peer(1), shard_peer(shards - 1)
@@ -208,9 +217,12 @@
         for index, (src, dst, peer, _, _) in enumerate(moves)
     ]
 
-    def launch(indices):
+    def launch(indices, only=None):
         for index in indices:
-            pl.when(moves[index][3])(copies[index].start)
+            ready_to = moves[index][3]
+            if only is not None:
+                ready_to = jnp.logical_and(ready_to, only)
+            pl.when(ready_to)(copies[index].start)
 
     def arrive(indices):
         for index in indices:
@@ -220,22 +232,24 @@
         for index in indices:
             pl.when(moves[index][3])(copies[index].wait_send)
 
-    pl.semaphore_wait(barrier, tiles + 1)
-    for group in cot_moves:
-        launch(group)
+    pl.semaphore_wait(barrier, tiles - 1 + near(1))
+    corner = (lax.rem(shard, 4) == 0, lax.rem(shard, 4) == 3)
     launch(cell_moves)
+    launch(cot_moves[0])
+    for group in cot_moves[1:]:
+        for index, held in zip(group, corner):
+            launch([index], jnp.logical_not(held) if HOLD else None)
     spans = []
     span = 1
-    while span * 2 < shards:
+    while span < shards - 1:
         spans.append(span)
         span *= 2
 
     def tell(index):
-        signal(ready.at[index], shard_peer(spans[index]))
-        signal(ready.at[index], shard_peer(shards - spans[index]))
+        around(ready.at[index], spans[index])
 
     def hear(index):
-        pl.semaphore_wait(ready.at[index], 2)
+        pl.semaphore_wait(ready.at[index], near(spans[index]))
 
     tell(0)
     for index in range(len(moves)):
@@ -287,12 +301,16 @@
     for index in range(1, len(spans)):
         if index == 1:
             tell(1)
-    sent = [0]
+    inner = lax.rem(shard + shard // 2, 2) == 1
 
     def send_acts(moment):
-        upto = min(ACTS_AT[moment] * len(act_order) // 8, len(act_order))
-        launch(act_order[sent[0] : upto])
-        sent[0] = upto
+        for kind, table in ((inner, ACTS_IN), (jnp.logical_not(inner), ACTS_AT)):
+            first, last = (
+                table[index] * len(act_order) // 16 if index >= 0 else 0
+                for index in (moment - 1, moment)
+            )
+            if last > first:
+                pl.when(kind)(functools.partial(launch, act_order[first:last]))
 
     send_acts(0)
 
@@ -359,11 +377,21 @@
             settle_frame(frame)
     for reach in range(1, REACH + 1):
         arrive(cot_moves[reach - 1])
+        if reach == 1 and HOLD == 1:
+            for group in cot_moves[1:]:
+                for index, held in zip(group, corner):
+                    launch([index], held)
+        if reach == REACH:
+            send_acts(1)
         for frame in range(count):
             if stage_of(frame) >= reach:
                 pull_halo(frame, reach)
                 if stage_of(frame) == reach:
                     settle_frame(frame)
+        if reach == 1 and HOLD == 2:
+            for group in cot_moves[1:]:
+                for index, held in zip(group, corner):
+                    launch([index], held)
 
     half = sums.shape[1] // tiles
     chunk = half // crew
@@ -393,6 +421,7 @@
             ),
         )
     launch(rim_moves)
+    send_acts(2)
 
     def out_forward(frame):
         joined = jnp.concatenate([flat(acts[frame + REACH - lag]) for lag in range(TAPS)], axis=1)
@@ -417,6 +446,8 @@
 
     def scatter(piece):
         settle(0, piece, pair_in.at[piece])
+        if piece == 0:
+            send_acts(3)
         value = sums[piece, mine, :]
         for index in range(tiles - 1):
             value = value + pair_in[piece, index]
@@ -435,7 +466,7 @@
 
     for piece in range(PIECES):
         scatter(piece)
-    send_acts(1)
+    send_acts(4)
 
     arrive(rim_moves)
     edge = columns(count * width, width, channels)
@@ -452,6 +483,7 @@
         grad_in[frame] = value.astype(KIND).reshape(height, width, channels)
 
     frames(0, count, input_grads)
+    send_acts(5)
 
     def share_mates(piece):
         settle(1, piece, shard_in.at[piece])
@@ -473,7 +505,7 @@
 
     for piece in range(PIECES):
         share_mates(piece)
-    send_acts(2)
+    send_acts(6)
 
     def gather(piece):
         value = mate_out[piece]
@@ -490,6 +522,7 @@
 
     for piece in range(PIECES):
         gather(piece)
+    send_acts(7)
 
     arrive(act_moves[0])
     outputs(1)
@@ -550,14 +583,14 @@
     count, height, width, channels = latent.shape
     positions = count * height * width * shards * tiles
     scale = 1.0 / math.sqrt(positions)
-    mates = 2 if shards % 2 == 0 else 1
+    mates = MATES if shards % MATES == 0 else 1
     crew = shards // mates
     rows = 4 * TAPS * channels // PIECES
     unit = 16 * tiles * crew
     padded = -(-rows // unit) * unit
     half = padded // tiles
     chunk = half // crew
-    stages = max(1, (shards - 1).bit_length() - 1)
+    stages = max(1, (shards - 2).bit_length())
     parts = PARTS if height % PARTS == 0 else 1
     moves = 4 + REACH * 2 + REACH * 2 * parts
     vmem = pl.BlockSpec(memory_space=pltpu.VMEM)

time: 46.2 us -> 42.2 us (0.913)
  Pallas kernels: 45.4 us -> 41.1 us
    pallas_call x1, Pallas kernels: 43.9 us -> 39.5 us  [body(): pl.pallas_call(functools.partial(kernel, tiles, shards, scale), out_shape...]
where the time goes in v3:
time: 42.2 us; the launch traced here: 41.7 us
  Pallas kernels  41.1 us (97%)
  between operations  0.64 us (2%)
    pallas_call x1, Pallas kernels, body(): pl.pallas_call(functools.partial(kernel, tiles, shards, scale), out_shape...  39.5 us
    pallas_call x1, Pallas kernels, deliver(): pl.pallas_call(deliver_kernel, out_shape=tuple((jax.ShapeDtypeStruct(valu...  1.56 us

profile of v3, /device:TPU:0, one launch (start us, length us, event | category | flops | bytes accessed | tf_op | source)
XLA Modules:
  0.0 41.7 jit_solution(15583018950493769603)
XLA Ops:
  0.6 39.5 %shard_map.92 = (bf16[4,4,160,128]{3,2,1,0:T(8,128)(2,1)S(1)}, bf16[4,4,160,128]{3,2,1,0:T(8,128)(2,1)S(1)}, bf16[4,4,160,128]{3,2,1,0:T(8,128)(2,1)S(1)}, f32[1152,128]{1,0:T(8,128)S(1)}, f32[384,128]{1,0:T(8,128)S(1)}) custom-call(bf16[4,4,160,128]{3,2,1,0:T(8,128)(2,1)} %latent_ref.1, bf16[4,4,160,128]{3,2,1,0:T(8,128)(2,1)} %fwd_ref.1, ...), custom_call_target="tpu_custom_call" | custom-call | tf_op jit(solution)/shard_map/pallas_call | solution.py:598
  40.1 1.6 %shard_map.93 = (bf16[4,4,160,128]{3,2,1,0:T(8,128)(2,1)}, bf16[4,4,160,128]{3,2,1,0:T(8,128)(2,1)}, bf16[4,4,160,128]{3,2,1,0:T(8,128)(2,1)}, f32[1152,128]{1,0:T(8,128)}, f32[384,128]{1,0:T(8,128)}) custom-call(bf16[4,4,160,128]{3,2,1,0:T(8,128)(2,1)S(1)} %get-tuple-element.15.refs_0_, bf16[4,4,160,128]{3,2,1,0:T(8,128)(2,1)S(1)} %get-tuple-element.16.refs_1_, ...), custom_call_target="tpu_custom_call" | custom-call | tf_op jit(solution)/shard_map/pallas_call | solution.py:571

commit v4 on v3

--- a/solution.py
+++ b/solution.py
@@ -12,12 +12,18 @@
 KIND = jnp.bfloat16
 TAPS = 3
 REACH = TAPS - 1
-PIECES = 1
-PARTS = 2
-MATES = 1
+PIECES = 2
+PARTS = 4
+MATES = 2
 HOLD = 1
-ACTS_AT = (0,0,4,4,8,8,12,16)
-ACTS_IN = (0,4,4,4,10,10,12,16)
+TURN = False
+SLABS = 1
+ACTS_INNER = (0,4,4,4,8,8,12,16)
+ACTS_SIDE = (0, 0, 4, 4, 8, 8, 12, 16)
+ACTS_INNER_ODD = (0,0,0,4,8,8,12,16)
+ACTS_SIDE_ODD = (0, 0, 4, 4, 8, 8, 12, 16)
+ACTS_FAR_ODD = (0, 0, 4, 4, 8, 8, 12, 16)
+ACTS_FAR = (0, 0, 4, 4, 8, 8, 12, 16)
 VMEM_LIMIT = 32 << 20
 
 
@@ -69,6 +75,10 @@
     return lax.dot_general(
         left, right, (((1,), (1,)), ((), ())), preferred_element_type=jnp.float32
     )
+
+
+def over(left, right):
+    return jnp.dot(left, right, preferred_element_type=jnp.float32)
 
 
 def contract(left, right):
@@ -97,6 +107,7 @@
     acts,
     gates,
     pulls,
+    tilted,
     wide,
     rim_out,
     rim_in,
@@ -115,6 +126,7 @@
     total,
     load_sem,
     ready,
+    clear,
     halo_send,
     halo_recv,
     sum_send,
@@ -205,7 +217,6 @@
                 move(acts.at[REACH + reach, cut], acts.at[count + REACH + reach, cut], earlier)
             )
         act_moves.append(group)
-    act_order = [index for group in act_moves for index in group]
 
     def remote(src, dst, send, recv, peer):
         return pltpu.make_async_remote_copy(
@@ -302,20 +313,38 @@
         if index == 1:
             tell(1)
     inner = lax.rem(shard + shard // 2, 2) == 1
+    outer = jnp.logical_not(inner)
+    even = lax.rem(tile, 2) == 0
+    odd = jnp.logical_not(even)
+    early = jnp.logical_and(inner, even)
+    act_ways = ([group[0::2] for group in act_moves], [group[1::2] for group in act_moves])
 
     def send_acts(moment):
-        for kind, table in ((inner, ACTS_IN), (jnp.logical_not(inner), ACTS_AT)):
-            first, last = (
-                table[index] * len(act_order) // 16 if index >= 0 else 0
-                for index in (moment - 1, moment)
-            )
-            if last > first:
-                pl.when(kind)(functools.partial(launch, act_order[first:last]))
+        before = max(0, moment - 1)
+        for groups, far in zip(act_ways, (corner[1], corner[0])):
+            order = [index for group in groups for index in group]
+            side = jnp.logical_and(outer, jnp.logical_not(far))
+            both = jnp.logical_and
+            for kind, table in (
+                (both(inner, even), ACTS_INNER),
+                (both(inner, odd), ACTS_INNER_ODD),
+                (both(side, even), ACTS_SIDE),
+                (both(side, odd), ACTS_SIDE_ODD),
+                (both(far, even), ACTS_FAR),
+                (both(far, odd), ACTS_FAR_ODD),
+            ):
+                first = table[before] * len(order) // 16 if moment else 0
+                last = table[moment] * len(order) // 16
+                if last > first:
+                    launch(order[first:last], kind)
 
     send_acts(0)
 
     def add_lag(lag, value):
         sums[0, block(lag), :] += value
+
+    def stage_of(frame):
+        return max(0, REACH - frame, REACH - (count - 1 - frame))
 
     def own_pull(frame):
         low = max(0, frame + REACH - (count - 1))
@@ -335,13 +364,14 @@
     loads[4].wait()
     for frame in range(count):
         own_pull(frame)
+        if stage_of(frame) == REACH:
+            spot = slice(min(frame, 1) * plane, (min(frame, 1) + 1) * plane)
+            tilted[: TAPS * channels, spot] = window(frame).T
+            tilted[TAPS * channels :, spot] = flat(acts[frame + REACH]).T
     for index in range(1, len(spans)):
         hear(index)
         if index + 1 < len(spans):
             tell(index + 1)
-
-    def stage_of(frame):
-        return max(0, REACH - frame, REACH - (count - 1 - frame))
 
     def halo_terms(frame, reach):
         terms = []
@@ -354,40 +384,79 @@
         return terms
 
     def pull_halo(frame, reach):
+        pull = pulls[frame]
         for lag, source, index in halo_terms(frame, reach):
             taken = flat(source[index])
-            pulls[frame] += across(taken, time_back[:, block(TAPS + lag)])
-            add_lag(lag, contract(flat(acts[frame + REACH]), taken))
-
-    def settle_frame(frame):
-        grad = (pulls[frame] * gates[frame]).astype(KIND)
+            pull = pull + across(taken, time_back[:, block(TAPS + lag)])
+        return pull
+
+    def lag_halo(frame, reach):
+        for lag, source, index in halo_terms(frame, reach):
+            add_lag(lag, contract(flat(acts[frame + REACH]), flat(source[index])))
+
+    def shift_frame(frame, pull):
+        grad = (pull * gates[frame]).astype(KIND)
         shifted = spread(grad.astype(jnp.float32), place, width)
         wide[frame, pl.ds(1, height)] = shifted.reshape(height, width, TAPS * channels)
         rim_out[0, frame] = grad[:width]
         rim_out[1, frame] = grad[plane - width :]
-        part = contract(window(frame), shifted)
+        return shifted
+
+    def add_taps(part):
         for row in range(TAPS):
             for col in range(TAPS):
                 tap = TAPS + row * TAPS + col
                 spot = block(tap % (4 * TAPS // PIECES))
                 sums[tap // (4 * TAPS // PIECES), spot, :] += part[block(row), block(col)]
 
+    def settle_frame(frame, pull):
+        add_taps(contract(window(frame), shift_frame(frame, pull)))
+
+    ends = [frame for frame in range(count) if stage_of(frame) == REACH]
+
+    def settle_ends():
+        shifted = [shift_frame(frame, pull_halo(frame, REACH)) for frame in ends]
+        halos = []
+        for frame in ends:
+            terms = halo_terms(frame, REACH)
+            assert len(terms) == 1 and terms[0][0] == REACH
+            halos.append(flat(terms[0][1][terms[0][2]]))
+        add_lag(REACH, over(tilted[TAPS * channels :, :], jnp.concatenate(halos, axis=0)))
+        add_taps(over(tilted[: TAPS * channels, :], jnp.concatenate(shifted, axis=0)))
+
     for frame in range(count):
         if stage_of(frame) == 0:
-            settle_frame(frame)
+            settle_frame(frame, pulls[frame])
+    cot_all = [index for group in cot_moves for index in group]
+
+    def drain():
+        leave(cot_all)
+        each(tiles, lambda step: signal(clear, tile_peer(step)))
+
+    def await_clear():
+        pl.semaphore_wait(clear, tiles - 1)
+
     for reach in range(1, REACH + 1):
+        if reach == REACH:
+            pl.when(inner)(drain)
+            pl.when(early)(await_clear)
+            send_acts(1)
         arrive(cot_moves[reach - 1])
         if reach == 1 and HOLD == 1:
             for group in cot_moves[1:]:
                 for index, held in zip(group, corner):
                     launch([index], held)
         if reach == REACH:
-            send_acts(1)
+            settle_ends()
+            break
         for frame in range(count):
             if stage_of(frame) >= reach:
-                pull_halo(frame, reach)
+                pull = pull_halo(frame, reach)
                 if stage_of(frame) == reach:
-                    settle_frame(frame)
+                    settle_frame(frame, pull)
+                else:
+                    pulls[frame] = pull
+                lag_halo(frame, reach)
         if reach == 1 and HOLD == 2:
             for group in cot_moves[1:]:
                 for index, held in zip(group, corner):
@@ -397,6 +466,16 @@
     chunk = half // crew
     rank = shard // mates
 
+    def chunk_of(seat):
+        if TURN and mates == 2 and crew % 4 == 0:
+            return seat + lax.rem(shard, 2) * (2 - 4 * lax.rem(seat // 2, 2))
+        return seat
+
+    seat = chunk_of(rank)
+    mate_rank = rank
+    if TURN and mates == 2 and crew % 4 == 0:
+        mate_rank = rank + 2 - 4 * lax.rem(rank // 2, 2)
+
     def settle(phase, piece, ref):
         spot = phase * PIECES + piece
         pltpu.make_async_copy(ref, ref, sum_send.at[spot]).wait()
@@ -407,7 +486,7 @@
         remote(src, dst, sum_send.at[spot], sum_recv.at[spot], peer).start()
 
     mine = at(tile * half, half)
-    own = at(tile * half + rank * chunk, chunk)
+    own = at(tile * half + seat * chunk, chunk)
 
     for piece in range(PIECES):
         each(
@@ -423,31 +502,36 @@
     launch(rim_moves)
     send_acts(2)
 
-    def out_forward(frame):
-        joined = jnp.concatenate([flat(acts[frame + REACH - lag]) for lag in range(TAPS)], axis=1)
-        value = flat(cells[frame, pl.ds(1, height)]).astype(jnp.float32)
-        value = value + jnp.dot(joined, time_ref[...], preferred_element_type=jnp.float32)
-        out_f[frame] = value.astype(KIND).reshape(height, width, channels)
-
-    def out_reverse(frame):
-        joined = jnp.concatenate([flat(acts[frame + REACH + lag]) for lag in range(TAPS)], axis=1)
-        value = flat(cells[frame, pl.ds(1, height)]).astype(jnp.float32)
-        value = value + jnp.dot(joined, time_ref[...], preferred_element_type=jnp.float32)
-        out_r[frame] = value.astype(KIND).reshape(height, width, channels)
+    def out_sum(value, frame, turn, lags):
+        joined = jnp.concatenate(
+            [flat(acts[frame + REACH + turn * lag]) for lag in lags], axis=1
+        )
+        weight = time_ref[lags[0] * channels : (lags[-1] + 1) * channels, :]
+        return value + jnp.dot(joined, weight, preferred_element_type=jnp.float32)
+
+    def out_base(frame):
+        return flat(cells[frame, pl.ds(1, height)]).astype(jnp.float32)
+
+    streams = ((out_f, -1, lambda frame: frame), (out_r, 1, lambda frame: count - 1 - frame))
 
     def outputs(reach):
-        for frame in range(count):
-            if max(0, REACH - frame) == reach:
-                out_forward(frame)
-            if max(0, REACH - (count - 1 - frame)) == reach:
-                out_reverse(frame)
+        for slot, (ref, turn, depth) in enumerate(streams):
+            for frame in range(count):
+                need = max(0, REACH - depth(frame))
+                if need == REACH and reach == REACH - 1:
+                    pulls[slot] = out_sum(out_base(frame), frame, turn, range(REACH))
+                if need != reach:
+                    continue
+                if reach == REACH:
+                    value = out_sum(pulls[slot], frame, turn, range(REACH, TAPS))
+                else:
+                    value = out_sum(out_base(frame), frame, turn, range(TAPS))
+                ref[frame] = value.astype(KIND).reshape(height, width, channels)
 
     outputs(0)
 
     def scatter(piece):
         settle(0, piece, pair_in.at[piece])
-        if piece == 0:
-            send_acts(3)
         value = sums[piece, mine, :]
         for index in range(tiles - 1):
             value = value + pair_in[piece, index]
@@ -458,12 +542,15 @@
             lambda step: pass_on(
                 1,
                 piece,
-                mid_out.at[piece, at(lax.rem(rank + step, crew) * chunk, chunk)],
+                mid_out.at[piece, at(chunk_of(lax.rem(rank + step, crew)) * chunk, chunk)],
                 shard_in.at[piece, step - 1],
                 crew_peer(step),
             ),
         )
 
+    pl.when(outer)(drain)
+    pl.when(jnp.logical_not(early))(await_clear)
+    send_acts(3)
     for piece in range(PIECES):
         scatter(piece)
     send_acts(4)
@@ -491,7 +578,7 @@
             0,
             crew - 1,
             lambda index, value: value + shard_in[piece, index].astype(jnp.float32),
-            mid[piece, at(rank * chunk, chunk), :],
+            mid[piece, at(seat * chunk, chunk), :],
         )
         mate_out[piece] = value
         if mates == 2:
@@ -500,7 +587,7 @@
                 piece,
                 mate_out.at[piece],
                 mate_in.at[piece],
-                {"tm": shard + 1 - 2 * lax.rem(shard, 2)},
+                {"tm": 2 * mate_rank + 1 - lax.rem(shard, 2)},
             )
 
     for piece in range(PIECES):
@@ -549,15 +636,21 @@
             grad_t[block(tap), :] = value
         else:
             grad_s[block(tap - TAPS), :] = value
-    leave(range(len(moves)))
+    leave([index for index in range(len(moves)) if index not in cot_all])
 
 
 def deliver_kernel(*refs):
     count = (len(refs) - 1) // 2
-    stores = [
-        pltpu.make_async_copy(refs[index], refs[count + index], refs[-1].at[index])
-        for index in range(count)
-    ]
+    stores = []
+    for index in range(count):
+        source, target = refs[index], refs[count + index]
+        cuts = SLABS if source.shape[0] % SLABS == 0 else 1
+        size = source.shape[0] // cuts
+        for cut in range(cuts):
+            rows = pl.ds(cut * size, size)
+            stores.append(
+                pltpu.make_async_copy(source.at[rows], target.at[rows], refs[-1].at[len(stores)])
+            )
     for store in stores:
         store.start()
     for store in stores:
@@ -573,7 +666,7 @@
         out_shape=tuple(jax.ShapeDtypeStruct(value.shape, value.dtype) for value in values),
         in_specs=[vmem] * count,
         out_specs=(hbm,) * count,
-        scratch_shapes=[pltpu.SemaphoreType.DMA((count,))],
+        scratch_shapes=[pltpu.SemaphoreType.DMA((count * SLABS,))],
         compiler_params=pltpu.CompilerParams(vmem_limit_bytes=VMEM_LIMIT),
     )(*(pltpu.with_memory_space_constraint(value, pltpu.VMEM) for value in values))
 
@@ -613,6 +706,7 @@
             pltpu.VMEM((count + 2 * REACH, height, width, channels), KIND),
             pltpu.VMEM((count, height * width, channels), jnp.float32),
             pltpu.VMEM((count, height * width, channels), jnp.float32),
+            pltpu.VMEM(((TAPS + 1) * channels, min(2, count) * height * width), KIND),
             pltpu.VMEM((count, height + 2, width, TAPS * channels), KIND),
             pltpu.VMEM((2, count, width, channels), KIND),
             pltpu.VMEM((2, count, width, channels), KIND),
@@ -631,6 +725,7 @@
             pltpu.VMEM((PIECES, padded, channels), KIND),
             pltpu.SemaphoreType.DMA((5,)),
             pltpu.SemaphoreType.REGULAR((stages,)),
+            pltpu.SemaphoreType.REGULAR,
             pltpu.SemaphoreType.DMA((moves,)),
             pltpu.SemaphoreType.DMA((moves,)),
             pltpu.SemaphoreType.DMA((5 * PIECES,)),

time: 42.2 us -> 41.9 us (level)
  no operation moved by 1% of the time
where the time goes in v4:
time: 41.9 us; the launch traced here: 41.7 us
  Pallas kernels  41.1 us (98%)
  between operations  0.64 us (2%)
    pallas_call x1, Pallas kernels, body(): pl.pallas_call(functools.partial(kernel, tiles, shards, scale), out_shape...  39.5 us
    pallas_call x1, Pallas kernels, deliver(): pl.pallas_call(deliver_kernel, out_shape=tuple((jax.ShapeDtypeStruct(valu...  1.56 us

profile of v4, /device:TPU:0, one launch (start us, length us, event | category | flops | bytes accessed | tf_op | source)
XLA Modules:
  0.0 41.7 jit_solution(13868683119650013788)
XLA Ops:
  0.6 39.5 %shard_map.92 = (bf16[4,4,160,128]{3,2,1,0:T(8,128)(2,1)S(1)}, bf16[4,4,160,128]{3,2,1,0:T(8,128)(2,1)S(1)}, bf16[4,4,160,128]{3,2,1,0:T(8,128)(2,1)S(1)}, f32[1152,128]{1,0:T(8,128)S(1)}, f32[384,128]{1,0:T(8,128)S(1)}) custom-call(bf16[4,4,160,128]{3,2,1,0:T(8,128)(2,1)} %latent_ref.1, bf16[4,4,160,128]{3,2,1,0:T(8,128)(2,1)} %fwd_ref.1, ...), custom_call_target="tpu_custom_call" | custom-call | tf_op jit(solution)/shard_map/pallas_call | solution.py:691
  40.1 1.6 %shard_map.93 = (bf16[4,4,160,128]{3,2,1,0:T(8,128)(2,1)}, bf16[4,4,160,128]{3,2,1,0:T(8,128)(2,1)}, bf16[4,4,160,128]{3,2,1,0:T(8,128)(2,1)}, f32[1152,128]{1,0:T(8,128)}, f32[384,128]{1,0:T(8,128)}) custom-call(bf16[4,4,160,128]{3,2,1,0:T(8,128)(2,1)S(1)} %get-tuple-element.15.refs_0_, bf16[4,4,160,128]{3,2,1,0:T(8,128)(2,1)S(1)} %get-tuple-element.16.refs_1_, ...), custom_call_target="tpu_custom_call" | custom-call | tf_op jit(solution)/shard_map/pallas_call | solution.py:664

commit v5 on v4

--- a/solution.py
+++ b/solution.py
@@ -15,12 +15,12 @@
 PIECES = 2
 PARTS = 4
 MATES = 2
-HOLD = 1
-TURN = False
+HOLD = 2
+TURN = True
 SLABS = 1
-ACTS_INNER = (0,4,4,4,8,8,12,16)
+ACTS_INNER = (0,4,4,4,10,10,12,16)
 ACTS_SIDE = (0, 0, 4, 4, 8, 8, 12, 16)
-ACTS_INNER_ODD = (0,0,0,4,8,8,12,16)
+ACTS_INNER_ODD = (0,0,0,4,10,10,12,16)
 ACTS_SIDE_ODD = (0, 0, 4, 4, 8, 8, 12, 16)
 ACTS_FAR_ODD = (0, 0, 4, 4, 8, 8, 12, 16)
 ACTS_FAR = (0, 0, 4, 4, 8, 8, 12, 16)

time: 41.9 us -> 41.4 us (0.988)
  Pallas kernels: 41.1 us -> 40.6 us
    pallas_call x1, Pallas kernels: 39.5 us -> 39.1 us  [body(): pl.pallas_call(functools.partial(kernel, tiles, shards, scale), out_shape...]
where the time goes in v5:
time: 41.4 us; the launch traced here: 41.3 us
  Pallas kernels  40.6 us (98%)
  between operations  0.64 us (2%)
    pallas_call x1, Pallas kernels, body(): pl.pallas_call(functools.partial(kernel, tiles, shards, scale), out_shape...  39.1 us
    pallas_call x1, Pallas kernels, deliver(): pl.pallas_call(deliver_kernel, out_shape=tuple((jax.ShapeDtypeStruct(valu...  1.56 us

profile of v5, /device:TPU:0, one launch (start us, length us, event | category | flops | bytes accessed | tf_op | source)
XLA Modules:
  0.0 41.3 jit_solution(388116133532668234)
XLA Ops:
  0.6 39.1 %shard_map.92 = (bf16[4,4,160,128]{3,2,1,0:T(8,128)(2,1)S(1)}, bf16[4,4,160,128]{3,2,1,0:T(8,128)(2,1)S(1)}, bf16[4,4,160,128]{3,2,1,0:T(8,128)(2,1)S(1)}, f32[1152,128]{1,0:T(8,128)S(1)}, f32[384,128]{1,0:T(8,128)S(1)}) custom-call(bf16[4,4,160,128]{3,2,1,0:T(8,128)(2,1)} %latent_ref.1, bf16[4,4,160,128]{3,2,1,0:T(8,128)(2,1)} %fwd_ref.1, ...), custom_call_target="tpu_custom_call" | custom-call | tf_op jit(solution)/shard_map/pallas_call | solution.py:691
  39.7 1.6 %shard_map.93 = (bf16[4,4,160,128]{3,2,1,0:T(8,128)(2,1)}, bf16[4,4,160,128]{3,2,1,0:T(8,128)(2,1)}, bf16[4,4,160,128]{3,2,1,0:T(8,128)(2,1)}, f32[1152,128]{1,0:T(8,128)}, f32[384,128]{1,0:T(8,128)}) custom-call(bf16[4,4,160,128]{3,2,1,0:T(8,128)(2,1)S(1)} %get-tuple-element.15.refs_0_, bf16[4,4,160,128]{3,2,1,0:T(8,128)(2,1)S(1)} %get-tuple-element.16.refs_1_, ...), custom_call_target="tpu_custom_call" | custom-call | tf_op jit(solution)/shard_map/pallas_call | solution.py:664
